TPU v7x, 128 devices: a whole 4x4x4 slice. The times are simulated.
128 devices in a mesh: face: 8 (over x, z_hi), tile: 16 (over z_lo, y, core).
Axes of the slice: x: 4, y: 4, z: 4 (z_hi: 2, z_lo: 2; z = z_hi * 2 + z_lo), core: 2. Of those that a mesh axis runs over, the one named last changes fastest.
Arguments:
- state_field: bfloat16 [4, 512, 1024, 256], P(None, 'face', 'tile'), may hold values from -6 to 6
- cotangent: bfloat16 [4, 512, 1024, 256], P(None, 'face', 'tile'), may hold values from -6 to 6
- depth_weight: float32 [9, 256], replicated, may hold values from -2 to 2
- depth_bias: float32 [256], replicated, may hold values from -3 to 3
- point_weight: bfloat16 [256, 256], replicated, may hold values from -0.375 to 0.375
- tile_links: int32 [128, 4], P(('face', 'tile')), may hold values from 0 to 127, as said below
- link_sides: int32 [128, 4], P(('face', 'tile')), may hold values from 0 to 3
- link_flips: int32 [128, 4], P(('face', 'tile')), may hold values from 0 to 1
- corner_masks: int32 [128, 4], P(('face', 'tile')), may hold values 0 or 1
Outputs:
- field_grad: bfloat16 [4, 512, 1024, 256], P(None, 'face', 'tile')
- depth_grad: float32 [9, 256], replicated
- bias_grad: float32 [256], replicated
- point_grad: float32 [256, 256], replicated
Inputs may be any that keep to these rules, and one draw needn't show every extreme that they name: Tile ids number the grid row by row, the row being the index along face. The four neighbours of a tile are the four tiles one step away along face or along tile with wrap-around, each exactly once. Links are mutual: if tile_links[a, s] = b and link_sides[a, s] = o then tile_links[b, o] = a, link_sides[b, o] = s and link_flips[b, o] = link_flips[a, s].
All inputs are finite; a program needn't handle non-finite values. No bound on the sum of `corner_masks` on one device may be relied on, other than what follows from the above.
Results may differ from a plain program's by a relative error of at most 0.0049.
Values may be sent and summed in bfloat16 or wider, within the bound.
No kernel may reach another device: no remote copies, remote signals or barrier semaphores. Data moves between devices by JAX's collectives and lax.ppermute only.
A program may use at most 192 MiB of HBM per device.

v0:
```python
import jax
import jax.numpy as jnp
from jax import lax
from jax.sharding import PartitionSpec as P

root_two_pi = 0.7978845608028654
cubic_coef = 0.044715


def with_halo(block, sides, width):
    for axis, dim in sides:
        count = lax.axis_size(axis)
        forward = [(i, i + 1) for i in range(count - 1)]
        forward.append((count - 1, 0))
        backward = [(target, source) for source, target in forward]
        low = lax.ppermute(
            lax.slice_in_dim(block, block.shape[dim] - width, None, axis=dim), axis, forward
        )
        high = lax.ppermute(lax.slice_in_dim(block, 0, width, axis=dim), axis, backward)
        block = jnp.concatenate([low, block, high], axis=dim)
    return block


def gelu_pair(hidden):
    inside = root_two_pi * (hidden + cubic_coef * hidden * hidden * hidden)
    tanh_val = jnp.tanh(inside)
    output = 0.5 * hidden * (1.0 + tanh_val)
    slope = 0.5 * (1.0 + tanh_val) + 0.5 * hidden * (1.0 - tanh_val * tanh_val) * root_two_pi * (
        1.0 + 3.0 * cubic_coef * hidden * hidden
    )
    return (output, slope)


def edge_rows(block):
    return jnp.stack([block[:, 0], block[:, :, -1], block[:, -1], block[:, :, 0]], axis=0)


def split_dirs(per_dir):
    return (
        jnp.stack([per_dir[0], per_dir[2]], axis=0),
        jnp.stack([per_dir[3], per_dir[1]], axis=0),
    )


def join_dirs(got_face, got_tile):
    return jnp.stack([got_face[0], got_tile[3], got_face[3], got_tile[0]], axis=0)


def padded_tile(block, rim_rows, cmask):
    rim32 = rim_rows.astype(jnp.float32)
    north_west = (cmask[0] * 0.5 * (rim32[0][:, 0] + rim32[3][:, 0])).astype(jnp.bfloat16)
    north_east = (cmask[1] * 0.5 * (rim32[0][:, -1] + rim32[1][:, 0])).astype(jnp.bfloat16)
    south_east = (cmask[2] * 0.5 * (rim32[1][:, -1] + rim32[2][:, -1])).astype(jnp.bfloat16)
    south_west = (cmask[3] * 0.5 * (rim32[2][:, 0] + rim32[3][:, -1])).astype(jnp.bfloat16)
    top_row = jnp.concatenate([north_west[:, None], rim_rows[0], north_east[:, None]], axis=1)
    low_row = jnp.concatenate([south_west[:, None], rim_rows[2], south_east[:, None]], axis=1)
    middle = jnp.concatenate([rim_rows[3][:, :, None], block, rim_rows[1][:, :, None]], axis=2)
    return jnp.concatenate([top_row[:, None], middle, low_row[:, None]], axis=1)


def rim_terms(tap_rows, ext_rows):
    inner_rows = ext_rows[:, :, 1:-1].astype(jnp.float32)
    zero_rows = jnp.zeros_like(inner_rows[:, :, :1])
    padded_rows = jnp.concatenate([zero_rows, inner_rows, zero_rows], axis=2)
    tap_first = tap_rows[:, 0][:, None, None, :]
    tap_middle = tap_rows[:, 1][:, None, None, :]
    tap_last = tap_rows[:, 2][:, None, None, :]
    result = (
        tap_first * padded_rows[:, :, 2:]
        + tap_middle * padded_rows[:, :, 1:-1]
        + tap_last * padded_rows[:, :, :-2]
    )
    result = result.at[:, :, 0].add(
        0.5 * tap_first[:, :, 0] * ext_rows[:, :, 0].astype(jnp.float32)
    )
    result = result.at[:, :, -1].add(
        0.5 * tap_last[:, :, 0] * ext_rows[:, :, -1].astype(jnp.float32)
    )
    return result


def shards(
    state_field,
    cotangent,
    depth_weight,
    depth_bias,
    point_weight,
    tile_links,
    link_sides,
    link_flips,
    corner_masks,
):
    batch_size, tile_side, unused_side, channels = state_field.shape
    face_count = lax.axis_size("face")
    tile_count = lax.axis_size("tile")
    face_pos = lax.axis_index("face")
    tile_pos = lax.axis_index("tile")
    toward = jnp.stack(
        [
            (face_pos - 1) % face_count * tile_count + tile_pos,
            face_pos * tile_count + (tile_pos + 1) % tile_count,
            (face_pos + 1) % face_count * tile_count + tile_pos,
            face_pos * tile_count + (tile_pos - 1) % tile_count,
        ]
    )
    matched = tile_links[0][:, None] == toward[None, :]
    counter = jnp.arange(4, dtype=jnp.int32)
    dir_of_side = jnp.sum(jnp.where(matched, counter[None, :], 0), axis=1)
    side_of_dir = jnp.sum(jnp.where(matched, counter[:, None], 0), axis=0)
    flip_side = (link_flips[0] == 1)[:, None, None, None]
    cmask = corner_masks[0].astype(jnp.float32)
    sending = jnp.take(edge_rows(state_field), side_of_dir, axis=0)
    along_face, along_tile = split_dirs(sending)
    got_face = with_halo(along_face, (("face", 0),), 1)
    got_tile = with_halo(along_tile, (("tile", 0),), 1)
    rim_rows = jnp.take(join_dirs(got_face, got_tile), dir_of_side, axis=0)
    rim_rows = jnp.where(flip_side, rim_rows[:, :, ::-1], rim_rows)
    padded = padded_tile(state_field, rim_rows, cmask)
    tap_table = depth_weight.reshape(3, 3, channels)
    hidden = jnp.zeros(state_field.shape, jnp.float32) + depth_bias
    for row_off in range(3):
        for col_off in range(3):
            hidden = hidden + tap_table[row_off, col_off] * padded[
                :, row_off : row_off + tile_side, col_off : col_off + tile_side
            ].astype(jnp.float32)
    output, slope = gelu_pair(hidden)
    act = output.astype(jnp.bfloat16)
    row_count = batch_size * tile_side * tile_side
    cot_rows = cotangent.reshape(row_count, channels)
    grad_act = lax.dot_general(
        cot_rows, point_weight, (((1,), (1,)), ((), ())), preferred_element_type=jnp.float32
    )
    grad_hidden = (grad_act.reshape(hidden.shape) * slope).astype(jnp.bfloat16)
    point_part = lax.dot_general(
        act.reshape(row_count, channels),
        cot_rows,
        (((0,), (0,)), ((), ())),
        preferred_element_type=jnp.float32,
    )
    grad32 = grad_hidden.astype(jnp.float32)
    depth_list = []
    for row_off in range(3):
        for col_off in range(3):
            window = padded[:, row_off : row_off + tile_side, col_off : col_off + tile_side].astype(
                jnp.float32
            )
            depth_list.append(jnp.sum(grad32 * window, axis=(0, 1, 2)))
    depth_part = jnp.stack(depth_list, axis=0)
    bias_part = jnp.sum(grad32, axis=(0, 1, 2))
    point_sum, depth_sum, bias_sum = lax.psum((point_part, depth_part, bias_part), ("face", "tile"))
    norm_scale = float(batch_size * tile_side * tile_side * face_count * tile_count) ** (-0.5)
    grad_padded = jnp.pad(grad32, ((0, 0), (1, 1), (1, 1), (0, 0)))
    inner_grad = jnp.zeros(state_field.shape, jnp.float32)
    for row_off in range(3):
        for col_off in range(3):
            inner_grad = (
                inner_grad
                + tap_table[row_off, col_off]
                * grad_padded[
                    :, 2 - row_off : 2 - row_off + tile_side, 2 - col_off : 2 - col_off + tile_side
                ]
            )
    side_taps = jnp.stack([tap_table[0], tap_table[:, 2], tap_table[2], tap_table[:, 0]], axis=0)
    low_corner = jnp.array([0, 1, 3, 0], dtype=jnp.int32)
    high_corner = jnp.array([1, 2, 2, 3], dtype=jnp.int32)
    mask_low = jnp.take(corner_masks[0], low_corner).astype(jnp.bfloat16)[:, None, None, None]
    mask_high = jnp.take(corner_masks[0], high_corner).astype(jnp.bfloat16)[:, None, None, None]
    hidden_edges = edge_rows(grad_hidden)
    ext_rows = jnp.concatenate(
        [hidden_edges[:, :, :1] * mask_low, hidden_edges, hidden_edges[:, :, -1:] * mask_high],
        axis=2,
    )
    rim_parts = rim_terms(side_taps, ext_rows)
    outgoing = jnp.take(rim_parts, side_of_dir, axis=0)
    part_face, part_tile = split_dirs(outgoing)
    back_face = with_halo(part_face.astype(jnp.bfloat16), (("face", 0),), 1).astype(part_face.dtype)
    back_tile = with_halo(part_tile.astype(jnp.bfloat16), (("tile", 0),), 1).astype(part_tile.dtype)
    incoming = jnp.take(join_dirs(back_face, back_tile), dir_of_side, axis=0)
    incoming = jnp.where(flip_side, incoming[:, :, ::-1], incoming)
    inner_grad = (
        inner_grad.at[:, 0]
        .add(incoming[0])
        .at[:, :, -1]
        .add(incoming[1])
        .at[:, -1]
        .add(incoming[2])
        .at[:, :, 0]
        .add(incoming[3])
    )
    field_grad = inner_grad.astype(jnp.bfloat16)
    return (field_grad, depth_sum * norm_scale, bias_sum * norm_scale, point_sum * norm_scale)


def solution(mesh):
    in_specs = (
        P(None, "face", "tile", None),
        P(None, "face", "tile", None),
        P(),
        P(),
        P(),
        P(("face", "tile"), None),
        P(("face", "tile"), None),
        P(("face", "tile"), None),
        P(("face", "tile"), None),
    )
    out_specs = (P(None, "face", "tile", None), P(), P(), P())
    return jax.shard_map(shards, mesh=mesh, in_specs=in_specs, out_specs=out_specs, check_vma=False)
```

profile of v0, /device:TPU:1, one launch (start us, length us, event | category | flops | bytes accessed | tf_op | source)
XLA Modules:
  0.0 391.2 jit_solution(6158489630904382677)
XLA Ops:
  9.3 11.6 %copy.60 = bf16[4,64,64,256]{3,1,0,2:T(8,128)(2,1)} copy(bf16[4,64,64,256]{3,2,1,0:T(8,128)(2,1)} %param.29) | data formatting | bytes 16777216 | tf_op args[0]
  22.7 4.5 %collective-permute-start = (bf16[1,4,64,256]{3,2,1,0:T(8,128)(2,1)S(1)}, bf16[1,4,64,256]{3,2,1,0:T(8,128)(2,1)S(1)}, u32[]{:S(2)}, u32[]{:S(2)}) collective-permute-start(bf16[1,4,64,256]{3,2,1,0:T(8,128)(2,1)S(1)} %get-tuple-element.148), channel_id=1, source_target_pairs={{0,16},{16,32},{32,48},{48,64},{64,80},{80,96},{96,112},{112,0},{1... | collective-permute-start | bytes 393224 | tf_op jit(solution)/shard_map/ppermute | solution.py:16
  27.2 2.1 collective-permute-start.3
  29.3 2.0 collective-permute-start.2
  39.6 16.4 %maximum_maximum_fusion = (bf16[4,65,66,256]{3,1,0,2:T(8,128)(2,1)S(1)}, bf16[4,65,66,256]{3,1,0,2:T(8,128)(2,1)}) fusion(bf16[4,64,1,256]{3,1,0,2:T(8,128)(2,1)S(1)} %get-tuple-element.145, bf16[4,64,64,256]{3,1,0,2:T(8,128)(2,1)} %copy.60, bf16[4,64,1,256]{3,1,0,2:T(8,128)(2,1)S(1)} %get-tuple-element.146, bf16[4,1,66,256]{3,1,0,2:T(2,128)(2,1)S(1)} %copy.64, ...), kind=kLoop, calls=%fused_computation.78 | loop fusion | flops 70287360 | bytes 26492928 | tf_op jit(solution)/shard_map/concatenate | solution.py:58
  56.0 35.1 %multiply_convert_fusion = (bf16[4,64,64,256]{3,1,0,2:T(8,128)(2,1)}, f32[4,64,64,256]{3,1,0,2:T(8,128)}) fusion(bf16[4,65,66,256]{3,1,0,2:T(8,128)(2,1)} %get-tuple-element.119, f32[256]{0:T(256)S(1)} %bitcast.133, f32[256]{0:T(256)S(1)} %bitcast.135, f32[256]{0:T(256)S(1)} %bitcast.137, bf16[4,64,1,256]{3,1,0,2:T(8,128)(2,1)S(1)} %get-tuple-element.145, ...), kind=kLoop, calls=%fused_computation.77 | loop fusion | flops 159383552 | bytes 84158464 | tf_op jit(solution)/shard_map/convert_element_type | solution.py:127
  91.1 16.0 %fusion.29 = f32[4,64,64,256]{3,1,0,2:T(8,128)} fusion(f32[4,64,64,256]{3,1,0,2:T(8,128)} %get-tuple-element.111), kind=kLoop, calls=%fused_computation.65 | loop fusion | flops 71303168 | bytes 33554432 | tf_op jit(solution)/shard_map/add | solution.py:28
  107.1 25.4 %fusion.39 = bf16[4,64,64,256]{3,2,1,0:T(8,128)(2,1)} fusion(f32[4,64,64,256]{3,1,0,2:T(8,128)} %fusion.29, bf16[4,64,64,256]{3,2,1,0:T(8,128)(2,1)} %param.30, bf16[256,256]{1,0:T(8,128)(2,1)S(1)} %copy-done), kind=kOutput, calls=%fused_computation.76 | convolution fusion | flops 2155872256 | bytes 33685504 | tf_op jit(solution)/shard_map/dot_general | solution.py:130
  132.5 35.5 %fusion.38 = (f32[256]{0:T(256)S(1)}, f32[256]{0:T(256)S(1)}, f32[256]{0:T(256)S(1)}, f32[256]{0:T(256)S(1)}, f32[256]{0:T(256)S(1)}, /*index=5*/f32[256]{0:T(25...) fusion(bf16[4,65,66,256]{3,1,0,2:T(8,128)(2,1)} %get-tuple-element.119, ...), kind=kLoop, calls=%fused_computation.74 | loop fusion | flops 130020864 | bytes 75769856 | tf_op jit(solution)/shard_map/reduce_sum | solution.py:147
  170.4 12.5 %fusion.78 = (bf16[4,64,64,256]{3,1,0,2:T(8,128)(2,1)}, f32[4,64,64,256]{3,1,0,2:T(8,128)}) fusion(bf16[4,64,64,256]{3,2,1,0:T(8,128)(2,1)} %fusion.39), kind=kLoop, calls=%fused_computation.198 | loop fusion | flops 4194304 | bytes 33554432 | tf_op jit(solution)/shard_map/convert_element_type | solution.py:133
  182.9 15.5 %fusion.43 = f32[256,256]{1,0:T(8,128)} fusion(bf16[4,64,64,256]{3,2,1,0:T(8,128)(2,1)} %param.30, bf16[4,64,64,256]{3,1,0,2:T(8,128)(2,1)} %get-tuple-element.110), kind=kOutput, calls=%fused_computation.87 | convolution fusion | flops 2147483648 | bytes 17039360 | tf_op jit(solution)/shard_map/dot_general | solution.py:134
  198.5 65.7 %all-reduce.3 = (f32[9,256]{1,0:T(8,128)S(1)}, f32[256]{0:T(256)S(1)}) all-reduce(f32[9,256]{1,0:T(8,128)S(1)} %stack.83, f32[256]{0:T(256)S(1)} %get-tuple-element.99), channel_id=1, replica_groups=mesh['face'=8,'tile'=16] {'face','tile'}, use_global_device_ids=true, to_apply=%region_11.15 | all-reduce | flops 2560 | bytes 20480 | tf_op jit(solution)/shard_map/psum | solution.py:150
  270.6 3.8 collective-permute-start.5
  274.4 51.6 %fusion.8 = f32[4,64,64,256]{3,1,0,2:T(8,128)} fusion(f32[4,64,64,256]{3,1,0,2:T(8,128)} %get-tuple-element.123, f32[256]{0:T(256)S(1)} %bitcast.134, f32[256]{0:T(256)S(1)} %bitcast.136, f32[256]{0:T(256)S(1)} %bitcast.138, f32[256]{0:T(256)S(1)} %bitcast.140, f32[256]{0:T(256)S(1)} %bitcast.142, f32[256]{0:T(256)S(1)} %bitcast.144, f32[256]{0:T(256)S(1)} %bitcast.146, ...), kind=kLoop, calls=%fused_computation.44 | loop fusion | flops 75497472 | bytes 41952256 | tf_op jit(solution)/shard_map/add | solution.py:157
  326.5 12.8 %all-reduce.6.cloned.1.call-done = f32[256,256]{1,0:T(8,128)} async-done(((f32[256,256]{1,0:T(8,128)}), f32[256,256]{1,0:T(8,128)}) %all-reduce.6.cloned.1.call-update) | async-done | bytes 262160 | tf_op jit(solution)/shard_map/psum | solution.py:150
  339.3 1.7 broadcast_multiply_fusion
  342.4 1.9 slice_add_fusion.1
  344.3 6.9 %scatter-add.24 = f32[4,64,64,256]{3,1,0,2:T(8,128)} dynamic-update-slice(f32[4,64,64,256]{3,1,0,2:T(8,128)} %fusion.8, f32[4,1,64,256]{3,1,0,2:T(1,128)S(1)} %slice_add_fusion.1, s32[]{:T(128)} %constant.237.clone.1, s32[]{:T(128)} %constant.237.clone.1, s32[]{:T(128)} %constant.237.clone.1, s32[]{:T(128)} %constant.237.clone.1) | dynamic-update-slice | bytes 524292 | tf_op jit(solution)/shard_map/scatter-add | solution.py:182
  351.2 1.7 fusion.55
  352.9 2.0 slice_add_fusion
  354.9 6.9 %scatter-add.26 = f32[4,64,64,256]{3,1,0,2:T(8,128)} dynamic-update-slice(f32[4,64,64,256]{3,1,0,2:T(8,128)} %fusion.55, f32[4,1,64,256]{3,1,0,2:T(1,128)S(1)} %slice_add_fusion, s32[]{:T(128)} %constant.237.clone.1, s32[]{:T(128)} %constant.249.clone.1, s32[]{:T(128)} %constant.237.clone.1, s32[]{:T(128)} %constant.237.clone.1) | dynamic-update-slice | bytes 524292 | tf_op jit(solution)/shard_map/scatter-add | solution.py:186
  361.8 1.7 fusion.53
  363.5 9.1 %convert_element_type.121 = bf16[4,64,64,256]{3,1,0,2:T(8,128)(2,1)} convert(f32[4,64,64,256]{3,1,0,2:T(8,128)} %fusion.53) | non-fusion elementwise | flops 4194304 | bytes 25165824 | tf_op jit(solution)/shard_map/convert_element_type | solution.py:190
  372.5 11.6 %copy.80 = bf16[4,64,64,256]{3,2,1,0:T(8,128)(2,1)} copy(bf16[4,64,64,256]{3,1,0,2:T(8,128)(2,1)} %convert_element_type.121) | data formatting | bytes 16777216
  (101 shorter events, 20.0 us)
Async XLA Ops:
  7.2 100.0 %copy-start = (bf16[256,256]{1,0:T(8,128)(2,1)S(1)}, bf16[256,256]{1,0:T(8,128)(2,1)}, u32[]{:S(2)}) copy-start(bf16[256,256]{1,0:T(8,128)(2,1)} %param.33) | copy-start | bytes 393220
  7.2 25.0 %copy-start.7 = (s32[4]{0:T(128)S(1)}, s32[4]{0:T(128)}, u32[]{:S(2)}) copy-start(s32[4]{0:T(128)} %constant.280) | copy-start | bytes 52
  7.2 25.0 %copy-start.6 = (s32[4]{0:T(128)S(1)}, s32[4]{0:T(128)}, u32[]{:S(2)}) copy-start(s32[4]{0:T(128)} %constant.281) | copy-start | bytes 52
  7.2 24.3 %copy-start.4 = (f32[9,256]{1,0:T(8,128)S(1)}, f32[9,256]{1,0:T(8,128)}, u32[]{:S(2)}) copy-start(f32[9,256]{1,0:T(8,128)} %param.31) | copy-start | bytes 27652
  7.2 24.3 %copy-start.8 = (s32[1,4]{1,0:T(1,128)S(1)}, s32[1,4]{1,0:T(1,128)}, u32[]{:S(2)}) copy-start(s32[1,4]{1,0:T(1,128)} %param.35) | copy-start | bytes 52
  7.2 24.3 %copy-start.2 = (s32[1,4]{1,0:T(1,128)S(1)}, s32[1,4]{1,0:T(1,128)}, u32[]{:S(2)}) copy-start(s32[1,4]{1,0:T(1,128)} %param.36) | copy-start | bytes 52
  7.2 332.0 %all-reduce.6.cloned.1.call-start = ((), (), s32[]{:S(2)}) async-start(), calls=%async_computation | async-start | bytes 524288 | tf_op jit(solution)/shard_map/psum | solution.py:150
  22.7 13.5 %collective-permute-start = (bf16[1,4,64,256]{3,2,1,0:T(8,128)(2,1)S(1)}, bf16[1,4,64,256]{3,2,1,0:T(8,128)(2,1)S(1)}, u32[]{:S(2)}, u32[]{:S(2)}) collective-permute-start(bf16[1,4,64,256]{3,2,1,0:T(8,128)(2,1)S(1)} %get-tuple-element.148), channel_id=1, source_target_pairs={{0,16},{16,32},{32,48},{48,64},{64,80},{80,96},{96,112},{112,0},{1... | collective-permute-start | bytes 393224 | tf_op jit(solution)/shard_map/ppermute | solution.py:16
  27.2 9.0 %collective-permute-start.3 = (bf16[1,4,64,256]{3,2,1,0:T(8,128)(2,1)S(1)}, bf16[1,4,64,256]{3,2,1,0:T(8,128)(2,1)S(1)}, u32[]{:S(2)}, u32[]{:S(2)}) collective-permute-start(bf16[1,4,64,256]{3,2,1,0:T(8,128)(2,1)S(1)} %get-tuple-element.149), channel_id=1, source_target_pairs={{0,1},{1,2},{2,3},{3,4},{4,5},{5,6},{6,7},{7,8},{8,9},{9,10},{10,1... | collective-permute-start | bytes 393224 | tf_op jit(solution)/shard_map/ppermute | solution.py:16
  29.3 8.2 %collective-permute-start.2 = (bf16[1,4,64,256]{3,2,1,0:T(8,128)(2,1)S(1)}, bf16[1,4,64,256]{3,2,1,0:T(8,128)(2,1)S(1)}, u32[]{:S(2)}, u32[]{:S(2)}) collective-permute-start(bf16[1,4,64,256]{3,2,1,0:T(8,128)(2,1)S(1)} %get-tuple-element.150), channel_id=1, source_target_pairs={{16,0},{32,16},{48,32},{64,48},{80,64},{96,80},{112,96},{0,112},{1... | collective-permute-start | bytes 393224 | tf_op jit(solution)/shard_map/ppermute | solution.py:19
  31.3 6.2 %collective-permute-start.1 = (bf16[1,4,64,256]{3,2,1,0:T(8,128)(2,1)S(1)}, bf16[1,4,64,256]{3,2,1,0:T(8,128)(2,1)S(1)}, u32[]{:S(2)}, u32[]{:S(2)}) collective-permute-start(bf16[1,4,64,256]{3,2,1,0:T(8,128)(2,1)S(1)} %get-tuple-element.151), channel_id=1, source_target_pairs={{1,0},{2,1},{3,2},{4,3},{5,4},{6,5},{7,6},{8,7},{9,8},{10,9},{11,1... | collective-permute-start | bytes 393224 | tf_op jit(solution)/shard_map/ppermute | solution.py:19
  38.9 17.2 %copy-start.5 = (f32[256]{0:T(256)S(1)}, f32[256]{0:T(256)}, u32[]{:S(2)}) copy-start(f32[256]{0:T(256)} %param.32) | copy-start | bytes 3076
  56.0 35.1 %copy-start.3 = (bf16[4,65,66,256]{3,1,0,2:T(8,128)(2,1)}, bf16[4,65,66,256]{3,1,0,2:T(8,128)(2,1)S(1)}, u32[]{:S(2)}) copy-start(bf16[4,65,66,256]{3,1,0,2:T(8,128)(2,1)S(1)} %get-tuple-element.118) | copy-start | bytes 26357764
  267.5 73.5 %collective-permute-start.4 = (bf16[1,4,64,256]{3,2,1,0:T(8,128)(2,1)S(1)}, bf16[1,4,64,256]{3,2,1,0:T(8,128)(2,1)S(1)}, u32[]{:S(2)}, u32[]{:S(2)}) collective-permute-start(bf16[1,4,64,256]{3,2,1,0:T(8,128)(2,1)S(1)} %get-tuple-element.138), channel_id=1, source_target_pairs={{0,16},{16,32},{32,48},{48,64},{64,80},{80,96},{96,112},{112,0},{1... | collective-permute-start | bytes 393224 | tf_op jit(solution)/shard_map/ppermute | solution.py:16
  268.9 72.1 %collective-permute-start.7 = (bf16[1,4,64,256]{3,2,1,0:T(8,128)(2,1)S(1)}, bf16[1,4,64,256]{3,2,1,0:T(8,128)(2,1)S(1)}, u32[]{:S(2)}, u32[]{:S(2)}) collective-permute-start(bf16[1,4,64,256]{3,2,1,0:T(8,128)(2,1)S(1)} %get-tuple-element.139), channel_id=1, source_target_pairs={{1,0},{2,1},{3,2},{4,3},{5,4},{6,5},{7,6},{8,7},{9,8},{10,9},{11,1... | collective-permute-start | bytes 393224 | tf_op jit(solution)/shard_map/ppermute | solution.py:19
  269.9 71.1 %collective-permute-start.6 = (bf16[1,4,64,256]{3,2,1,0:T(8,128)(2,1)S(1)}, bf16[1,4,64,256]{3,2,1,0:T(8,128)(2,1)S(1)}, u32[]{:S(2)}, u32[]{:S(2)}) collective-permute-start(bf16[1,4,64,256]{3,2,1,0:T(8,128)(2,1)S(1)} %get-tuple-element.140), channel_id=1, source_target_pairs={{0,1},{1,2},{2,3},{3,4},{4,5},{5,6},{6,7},{7,8},{8,9},{9,10},{10,1... | collective-permute-start | bytes 393224 | tf_op jit(solution)/shard_map/ppermute | solution.py:16
  270.6 70.4 %collective-permute-start.5 = (bf16[1,4,64,256]{3,2,1,0:T(8,128)(2,1)S(1)}, bf16[1,4,64,256]{3,2,1,0:T(8,128)(2,1)S(1)}, u32[]{:S(2)}, u32[]{:S(2)}) collective-permute-start(bf16[1,4,64,256]{3,2,1,0:T(8,128)(2,1)S(1)} %get-tuple-element.141), channel_id=1, source_target_pairs={{16,0},{32,16},{48,32},{64,48},{80,64},{96,80},{112,96},{0,112},{1... | collective-permute-start | bytes 393224 | tf_op jit(solution)/shard_map/ppermute | solution.py:19
  361.8 22.4 %copy-start.1 = (bf16[256,256]{1,0:T(8,128)(2,1)S(1)}, bf16[256,256]{1,0:T(8,128)(2,1)}, u32[]{:S(2)}) copy-start(bf16[256,256]{1,0:T(8,128)(2,1)} %param.33) | copy-start | bytes 393220
Sparse Core Ops, SparseCore 0:
  198.6 140.6 all-reduce.5
where the time goes:
time: 398 us; the launch traced here: 391 us
  other arithmetic  189 us (47%)
  blocking collectives  65.7 us (17%)
  local copies, waits for them, and re-layouts  48 us (12%)
  matrix products  40.9 us (10%)
  between operations  17.4 us (4%)
  starting transfers between devices  15.7 us (4%)
  waiting for transfers between devices  14.1 us (4%)
    psum x1, blocking collectives, shards(): lax.psum((point_part, depth_part, bias_part), ('face', 'tile'))  65.7 us
    add x1, other arithmetic, shards(): inner_grad + tap_table[row_off, col_off] * grad_padded[:, 2 - row_off:2 -...  51.6 us
    reduce_sum x1, other arithmetic, shards(): depth_list.append(jnp.sum(grad32 * window, axis=(0, 1, 2)))  35.5 us
    convert_element_type x1, other arithmetic, shards(): act = output.astype(jnp.bfloat16)  35.1 us
    dot_general x1, matrix products, shards(): lax.dot_general(cot_rows, point_weight, (((1,), (1,)), ((), ())), preferr...  25.4 us
    unnamed x26, local copies, waits for them, and re-layouts  23.3 us
    concatenate x1, other arithmetic, padded_tile(): return jnp.concatenate([top_row[:, None], middle, low_row[:, None]], axis=1)  16.4 us
    add x1, other arithmetic, gelu_pair(): 0.5 * (1.0 + tanh_val)  16 us
  transfers between devices with their start and end apart: 9, of which 2 were waited for; matrix products, arithmetic and copies ran while one was open for 15% of the time, Pallas kernels for 0%

commit v1 on v0

--- a/solution.py
+++ b/solution.py
@@ -147,7 +147,9 @@
             depth_list.append(jnp.sum(grad32 * window, axis=(0, 1, 2)))
     depth_part = jnp.stack(depth_list, axis=0)
     bias_part = jnp.sum(grad32, axis=(0, 1, 2))
-    point_sum, depth_sum, bias_sum = lax.psum((point_part, depth_part, bias_part), ("face", "tile"))
+    point_sum, depth_sum, bias_sum = lax.psum(
+        lax.psum((point_part, depth_part, bias_part), "face"), "tile"
+    )
     norm_scale = float(batch_size * tile_side * tile_side * face_count * tile_count) ** (-0.5)
     grad_padded = jnp.pad(grad32, ((0, 0), (1, 1), (1, 1), (0, 0)))
     inner_grad = jnp.zeros(state_field.shape, jnp.float32)

time: 398 us -> 496 us (1.25)
  waiting for transfers between devices: 14.1 us -> 82.7 us
  blocking collectives: 65.7 us -> 91.6 us
    psum x1 -> x2, waiting for transfers between devices: 12.8 us -> 81.4 us  [the longest x1 81.4 us: shards(): lax.psum(lax.psum((point_part, depth_part, bias_part), 'face'), 'tile')]
    psum x1 -> x2, blocking collectives: 65.7 us -> 91.6 us  [the longest x1 58.2 us: shards(): lax.psum(lax.psum((point_part, depth_part, bias_part), 'face'), 'tile')]
  transfers between devices with their start and end apart: 9 -> 10, of which waited for: 2 -> 2; matrix products, arithmetic and copies ran while one was open for 15% -> 21% of each run, Pallas kernels for 0% -> 0%
where the time goes in v1:
time: 496 us; the launch traced here: 489 us
  other arithmetic  190 us (38%)
  blocking collectives  91.6 us (18%)
  waiting for transfers between devices  82.7 us (17%)
  local copies, waits for them, and re-layouts  48.2 us (10%)
  matrix products  40.9 us (8%)
  starting transfers between devices  18.4 us (4%)
  between operations  17.4 us (4%)
    psum x1, waiting for transfers between devices, shards(): lax.psum(lax.psum((point_part, depth_part, bias_part), 'face'), 'tile')  81.4 us
    psum x1, blocking collectives, shards(): lax.psum(lax.psum((point_part, depth_part, bias_part), 'face'), 'tile')  58.2 us
    add x1, other arithmetic, shards(): inner_grad + tap_table[row_off, col_off] * grad_padded[:, 2 - row_off:2 -...  51.4 us
    reduce_sum x1, other arithmetic, shards(): depth_list.append(jnp.sum(grad32 * window, axis=(0, 1, 2)))  36.1 us
    convert_element_type x1, other arithmetic, shards(): act = output.astype(jnp.bfloat16)  35.2 us
    psum x1, blocking collectives, shards(): lax.psum((point_part, depth_part, bias_part), 'face')  33.4 us
    dot_general x1, matrix products, shards(): lax.dot_general(cot_rows, point_weight, (((1,), (1,)), ((), ())), preferr...  25.4 us
    unnamed x26, local copies, waits for them, and re-layouts  23.3 us
  transfers between devices with their start and end apart: 10, of which 2 were waited for; matrix products, arithmetic and copies ran while one was open for 21% of the time, Pallas kernels for 0%

profile of v1, /device:TPU:1, one launch (start us, length us, event | category | flops | bytes accessed | tf_op | source)
XLA Modules:
  0.0 489.2 jit_solution(7660974538862310796)
XLA Ops:
  9.3 11.6 %copy.60 = bf16[4,64,64,256]{3,1,0,2:T(8,128)(2,1)} copy(bf16[4,64,64,256]{3,2,1,0:T(8,128)(2,1)} %param.29) | data formatting | bytes 16777216 | tf_op args[0]
  22.7 4.5 collective-permute-start
  27.2 2.1 collective-permute-start.3
  29.3 2.0 collective-permute-start.2
  39.6 16.4 %maximum_maximum_fusion = (bf16[4,65,66,256]{3,1,0,2:T(8,128)(2,1)S(1)}, bf16[4,65,66,256]{3,1,0,2:T(8,128)(2,1)}) fusion(bf16[4,64,1,256]{3,1,0,2:T(8,128)(2,1)S(1)} %get-tuple-element.147, bf16[4,64,64,256]{3,1,0,2:T(8,128)(2,1)} %copy.60, bf16[4,64,1,256]{3,1,0,2:T(8,128)(2,1)S(1)} %get-tuple-element.148, bf16[4,1,66,256]{3,1,0,2:T(2,128)(2,1)S(1)} %copy.64, ...), kind=kLoop, calls=%fused_computation.78 | loop fusion | flops 70287360 | bytes 26492928 | tf_op jit(solution)/shard_map/concatenate | solution.py:58
  56.0 35.2 %multiply_convert_fusion = (bf16[4,64,64,256]{3,1,0,2:T(8,128)(2,1)}, f32[4,64,64,256]{3,1,0,2:T(8,128)}) fusion(bf16[4,65,66,256]{3,1,0,2:T(8,128)(2,1)} %get-tuple-element.121, f32[256]{0:T(256)S(1)} %bitcast.133, f32[256]{0:T(256)S(1)} %bitcast.135, f32[256]{0:T(256)S(1)} %bitcast.137, bf16[4,64,1,256]{3,1,0,2:T(8,128)(2,1)S(1)} %get-tuple-element.147, ...), kind=kLoop, calls=%fused_computation.77 | loop fusion | flops 159383552 | bytes 84158464 | tf_op jit(solution)/shard_map/convert_element_type | solution.py:127
  91.2 16.0 %fusion.29 = f32[4,64,64,256]{3,1,0,2:T(8,128)} fusion(f32[4,64,64,256]{3,1,0,2:T(8,128)} %get-tuple-element.113), kind=kLoop, calls=%fused_computation.65 | loop fusion | flops 71303168 | bytes 33554432 | tf_op jit(solution)/shard_map/add | solution.py:28
  107.2 25.4 %fusion.39 = bf16[4,64,64,256]{3,2,1,0:T(8,128)(2,1)} fusion(f32[4,64,64,256]{3,1,0,2:T(8,128)} %fusion.29, bf16[4,64,64,256]{3,2,1,0:T(8,128)(2,1)} %param.30, bf16[256,256]{1,0:T(8,128)(2,1)S(1)} %copy-done), kind=kOutput, calls=%fused_computation.76 | convolution fusion | flops 2155872256 | bytes 33685504 | tf_op jit(solution)/shard_map/dot_general | solution.py:130
  132.6 36.1 %fusion.38 = (f32[256]{0:T(256)S(1)}, f32[256]{0:T(256)S(1)}, f32[256]{0:T(256)S(1)}, f32[256]{0:T(256)S(1)}, f32[256]{0:T(256)S(1)}, /*index=5*/f32[256]{0:T(25...) fusion(bf16[4,65,66,256]{3,1,0,2:T(8,128)(2,1)} %get-tuple-element.121, ...), kind=kLoop, calls=%fused_computation.74 | loop fusion | flops 130020864 | bytes 75769856 | tf_op jit(solution)/shard_map/reduce_sum | solution.py:147
  171.1 12.5 %fusion.78 = (bf16[4,64,64,256]{3,1,0,2:T(8,128)(2,1)}, f32[4,64,64,256]{3,1,0,2:T(8,128)}) fusion(bf16[4,64,64,256]{3,2,1,0:T(8,128)(2,1)} %fusion.39), kind=kLoop, calls=%fused_computation.198 | loop fusion | flops 4194304 | bytes 33554432 | tf_op jit(solution)/shard_map/convert_element_type | solution.py:133
  183.6 15.5 %fusion.43 = f32[256,256]{1,0:T(8,128)} fusion(bf16[4,64,64,256]{3,2,1,0:T(8,128)(2,1)} %param.30, bf16[4,64,64,256]{3,1,0,2:T(8,128)(2,1)} %get-tuple-element.112), kind=kOutput, calls=%fused_computation.87 | convolution fusion | flops 2147483648 | bytes 17039360 | tf_op jit(solution)/shard_map/dot_general | solution.py:134
  199.2 33.4 %all-reduce.4 = (f32[9,256]{1,0:T(8,128)S(1)}, f32[256]{0:T(256)S(1)}) all-reduce(f32[9,256]{1,0:T(8,128)S(1)} %stack.83, f32[256]{0:T(256)S(1)} %get-tuple-element.99), channel_id=1, replica_groups=mesh['face'=8,'tile'=16] {'face'}, use_global_device_ids=true, to_apply=%region_11.15 | all-reduce | flops 2560 | bytes 20480 | tf_op jit(solution)/shard_map/psum | solution.py:151
  232.7 58.2 %all-reduce.3 = (f32[9,256]{1,0:T(8,128)S(1)}, f32[256]{0:T(256)S(1)}) all-reduce(f32[9,256]{1,0:T(8,128)S(1)} %get-tuple-element.110, f32[256]{0:T(256)S(1)} %get-tuple-element.111), channel_id=1, replica_groups=mesh['face'=8,'tile'=16] {'tile'}, use_global_device_ids=true, to_apply=%region_12.16 | all-reduce | flops 2560 | bytes 20480 | tf_op jit(solution)/shard_map/psum | solution.py:150
  294.4 4.2 collective-permute-start.7
  298.6 5.3 %collective-permute-start.5 = (bf16[1,4,64,256]{3,2,1,0:T(8,128)(2,1)S(1)}, bf16[1,4,64,256]{3,2,1,0:T(8,128)(2,1)S(1)}, u32[]{:S(2)}, u32[]{:S(2)}) collective-permute-start(bf16[1,4,64,256]{3,2,1,0:T(8,128)(2,1)S(1)} %get-tuple-element.143), channel_id=1, source_target_pairs={{16,0},{32,16},{48,32},{64,48},{80,64},{96,80},{112,96},{0,112},{1... | collective-permute-start | bytes 393224 | tf_op jit(solution)/shard_map/ppermute | solution.py:19
  303.9 51.4 %fusion.8 = f32[4,64,64,256]{3,1,0,2:T(8,128)} fusion(f32[4,64,64,256]{3,1,0,2:T(8,128)} %get-tuple-element.125, f32[256]{0:T(256)S(1)} %bitcast.134, f32[256]{0:T(256)S(1)} %bitcast.136, f32[256]{0:T(256)S(1)} %bitcast.138, f32[256]{0:T(256)S(1)} %bitcast.140, f32[256]{0:T(256)S(1)} %bitcast.142, f32[256]{0:T(256)S(1)} %bitcast.144, f32[256]{0:T(256)S(1)} %bitcast.146, ...), kind=kLoop, calls=%fused_computation.44 | loop fusion | flops 75497472 | bytes 41952256 | tf_op jit(solution)/shard_map/add | solution.py:159
  357.3 1.9 slice_add_fusion.1
  359.2 6.8 %scatter-add.24 = f32[4,64,64,256]{3,1,0,2:T(8,128)} dynamic-update-slice(f32[4,64,64,256]{3,1,0,2:T(8,128)} %fusion.8, f32[4,1,64,256]{3,1,0,2:T(1,128)S(1)} %slice_add_fusion.1, s32[]{:T(128)} %constant.237.clone.1, s32[]{:T(128)} %constant.237.clone.1, s32[]{:T(128)} %constant.237.clone.1, s32[]{:T(128)} %constant.237.clone.1) | dynamic-update-slice | bytes 524292 | tf_op jit(solution)/shard_map/scatter-add | solution.py:184
  367.7 2.0 slice_add_fusion
  369.8 6.9 %scatter-add.26 = f32[4,64,64,256]{3,1,0,2:T(8,128)} dynamic-update-slice(f32[4,64,64,256]{3,1,0,2:T(8,128)} %fusion.55, f32[4,1,64,256]{3,1,0,2:T(1,128)S(1)} %slice_add_fusion, s32[]{:T(128)} %constant.237.clone.1, s32[]{:T(128)} %constant.249.clone.1, s32[]{:T(128)} %constant.237.clone.1, s32[]{:T(128)} %constant.237.clone.1) | dynamic-update-slice | bytes 524292 | tf_op jit(solution)/shard_map/scatter-add | solution.py:188
  376.6 1.7 fusion.53
  378.3 9.1 %convert_element_type.121 = bf16[4,64,64,256]{3,1,0,2:T(8,128)(2,1)} convert(f32[4,64,64,256]{3,1,0,2:T(8,128)} %fusion.53) | non-fusion elementwise | flops 4194304 | bytes 25165824 | tf_op jit(solution)/shard_map/convert_element_type | solution.py:192
  387.5 11.7 %copy.80 = bf16[4,64,64,256]{3,2,1,0:T(8,128)(2,1)} copy(bf16[4,64,64,256]{3,1,0,2:T(8,128)(2,1)} %convert_element_type.121) | data formatting | bytes 16777216
  399.1 81.4 %all-reduce.10.cloned.1.call-done = f32[256,256]{1,0:T(8,128)} async-done(((f32[256,256]{1,0:T(8,128)}), f32[256,256]{1,0:T(8,128)}) %all-reduce.10.cloned.1.call-update) | async-done | bytes 262160 | tf_op jit(solution)/shard_map/psum | solution.py:150
  (105 shorter events, 20.5 us)
Async XLA Ops:
  7.2 100.0 %copy-start = (bf16[256,256]{1,0:T(8,128)(2,1)S(1)}, bf16[256,256]{1,0:T(8,128)(2,1)}, u32[]{:S(2)}) copy-start(bf16[256,256]{1,0:T(8,128)(2,1)} %param.33) | copy-start | bytes 393220
  7.2 25.1 %copy-start.7 = (s32[4]{0:T(128)S(1)}, s32[4]{0:T(128)}, u32[]{:S(2)}) copy-start(s32[4]{0:T(128)} %constant.280) | copy-start | bytes 52
  7.2 25.1 %copy-start.6 = (s32[4]{0:T(128)S(1)}, s32[4]{0:T(128)}, u32[]{:S(2)}) copy-start(s32[4]{0:T(128)} %constant.281) | copy-start | bytes 52
  7.2 24.3 %copy-start.4 = (f32[9,256]{1,0:T(8,128)S(1)}, f32[9,256]{1,0:T(8,128)}, u32[]{:S(2)}) copy-start(f32[9,256]{1,0:T(8,128)} %param.31) | copy-start | bytes 27652
  7.2 24.3 %copy-start.8 = (s32[1,4]{1,0:T(1,128)S(1)}, s32[1,4]{1,0:T(1,128)}, u32[]{:S(2)}) copy-start(s32[1,4]{1,0:T(1,128)} %param.35) | copy-start | bytes 52
  7.2 24.3 %copy-start.2 = (s32[1,4]{1,0:T(1,128)S(1)}, s32[1,4]{1,0:T(1,128)}, u32[]{:S(2)}) copy-start(s32[1,4]{1,0:T(1,128)} %param.36) | copy-start | bytes 52
  7.2 360.5 %all-reduce.8.cloned.1.call-start = ((), (), s32[]{:S(2)}) async-start(), calls=%async_computation | async-start | bytes 524288 | tf_op jit(solution)/shard_map/psum | solution.py:151
  22.7 13.6 %collective-permute-start = (bf16[1,4,64,256]{3,2,1,0:T(8,128)(2,1)S(1)}, bf16[1,4,64,256]{3,2,1,0:T(8,128)(2,1)S(1)}, u32[]{:S(2)}, u32[]{:S(2)}) collective-permute-start(bf16[1,4,64,256]{3,2,1,0:T(8,128)(2,1)S(1)} %get-tuple-element.150), channel_id=1, source_target_pairs={{0,16},{16,32},{32,48},{48,64},{64,80},{80,96},{96,112},{112,0},{1... | collective-permute-start | bytes 393224 | tf_op jit(solution)/shard_map/ppermute | solution.py:16
  27.2 9.1 %collective-permute-start.3 = (bf16[1,4,64,256]{3,2,1,0:T(8,128)(2,1)S(1)}, bf16[1,4,64,256]{3,2,1,0:T(8,128)(2,1)S(1)}, u32[]{:S(2)}, u32[]{:S(2)}) collective-permute-start(bf16[1,4,64,256]{3,2,1,0:T(8,128)(2,1)S(1)} %get-tuple-element.151), channel_id=1, source_target_pairs={{0,1},{1,2},{2,3},{3,4},{4,5},{5,6},{6,7},{7,8},{8,9},{9,10},{10,1... | collective-permute-start | bytes 393224 | tf_op jit(solution)/shard_map/ppermute | solution.py:16
  29.3 8.2 %collective-permute-start.2 = (bf16[1,4,64,256]{3,2,1,0:T(8,128)(2,1)S(1)}, bf16[1,4,64,256]{3,2,1,0:T(8,128)(2,1)S(1)}, u32[]{:S(2)}, u32[]{:S(2)}) collective-permute-start(bf16[1,4,64,256]{3,2,1,0:T(8,128)(2,1)S(1)} %get-tuple-element.152), channel_id=1, source_target_pairs={{16,0},{32,16},{48,32},{64,48},{80,64},{96,80},{112,96},{0,112},{1... | collective-permute-start | bytes 393224 | tf_op jit(solution)/shard_map/ppermute | solution.py:19
  31.3 6.2 %collective-permute-start.1 = (bf16[1,4,64,256]{3,2,1,0:T(8,128)(2,1)S(1)}, bf16[1,4,64,256]{3,2,1,0:T(8,128)(2,1)S(1)}, u32[]{:S(2)}, u32[]{:S(2)}) collective-permute-start(bf16[1,4,64,256]{3,2,1,0:T(8,128)(2,1)S(1)} %get-tuple-element.153), channel_id=1, source_target_pairs={{1,0},{2,1},{3,2},{4,3},{5,4},{6,5},{7,6},{8,7},{9,8},{10,9},{11,1... | collective-permute-start | bytes 393224 | tf_op jit(solution)/shard_map/ppermute | solution.py:19
  38.9 17.1 %copy-start.5 = (f32[256]{0:T(256)S(1)}, f32[256]{0:T(256)}, u32[]{:S(2)}) copy-start(f32[256]{0:T(256)} %param.32) | copy-start | bytes 3076
  56.0 35.2 %copy-start.3 = (bf16[4,65,66,256]{3,1,0,2:T(8,128)(2,1)}, bf16[4,65,66,256]{3,1,0,2:T(8,128)(2,1)S(1)}, u32[]{:S(2)}) copy-start(bf16[4,65,66,256]{3,1,0,2:T(8,128)(2,1)S(1)} %get-tuple-element.120) | copy-start | bytes 26357764
  199.2 281.3 %all-reduce.10.cloned.1.call-start = ((), (), s32[]{:S(2)}) async-start(), calls=%async_computation.1 | async-start | bytes 524288 | tf_op jit(solution)/shard_map/psum | solution.py:150
  294.3 61.5 %collective-permute-start.4 = (bf16[1,4,64,256]{3,2,1,0:T(8,128)(2,1)S(1)}, bf16[1,4,64,256]{3,2,1,0:T(8,128)(2,1)S(1)}, u32[]{:S(2)}, u32[]{:S(2)}) collective-permute-start(bf16[1,4,64,256]{3,2,1,0:T(8,128)(2,1)S(1)} %get-tuple-element.140), channel_id=1, source_target_pairs={{0,16},{16,32},{32,48},{48,64},{64,80},{80,96},{96,112},{112,0},{1... | collective-permute-start | bytes 393224 | tf_op jit(solution)/shard_map/ppermute | solution.py:16
  294.4 61.4 %collective-permute-start.7 = (bf16[1,4,64,256]{3,2,1,0:T(8,128)(2,1)S(1)}, bf16[1,4,64,256]{3,2,1,0:T(8,128)(2,1)S(1)}, u32[]{:S(2)}, u32[]{:S(2)}) collective-permute-start(bf16[1,4,64,256]{3,2,1,0:T(8,128)(2,1)S(1)} %get-tuple-element.141), channel_id=1, source_target_pairs={{1,0},{2,1},{3,2},{4,3},{5,4},{6,5},{7,6},{8,7},{9,8},{10,9},{11,1... | collective-permute-start | bytes 393224 | tf_op jit(solution)/shard_map/ppermute | solution.py:19
  298.6 57.2 %collective-permute-start.6 = (bf16[1,4,64,256]{3,2,1,0:T(8,128)(2,1)S(1)}, bf16[1,4,64,256]{3,2,1,0:T(8,128)(2,1)S(1)}, u32[]{:S(2)}, u32[]{:S(2)}) collective-permute-start(bf16[1,4,64,256]{3,2,1,0:T(8,128)(2,1)S(1)} %get-tuple-element.142), channel_id=1, source_target_pairs={{0,1},{1,2},{2,3},{3,4},{4,5},{5,6},{6,7},{7,8},{8,9},{9,10},{10,1... | collective-permute-start | bytes 393224 | tf_op jit(solution)/shard_map/ppermute | solution.py:16
  298.6 57.3 %collective-permute-start.5 = (bf16[1,4,64,256]{3,2,1,0:T(8,128)(2,1)S(1)}, bf16[1,4,64,256]{3,2,1,0:T(8,128)(2,1)S(1)}, u32[]{:S(2)}, u32[]{:S(2)}) collective-permute-start(bf16[1,4,64,256]{3,2,1,0:T(8,128)(2,1)S(1)} %get-tuple-element.143), channel_id=1, source_target_pairs={{16,0},{32,16},{48,32},{64,48},{80,64},{96,80},{112,96},{0,112},{1... | collective-permute-start | bytes 393224 | tf_op jit(solution)/shard_map/ppermute | solution.py:19
  376.6 105.6 %copy-start.1 = (bf16[256,256]{1,0:T(8,128)(2,1)S(1)}, bf16[256,256]{1,0:T(8,128)(2,1)}, u32[]{:S(2)}) copy-start(bf16[256,256]{1,0:T(8,128)(2,1)} %param.33) | copy-start | bytes 393220
Sparse Core Ops, SparseCore 0:
  199.3 77.9 all-reduce.7
  367.9 112.5 all-reduce.9
